TPU v7x, 128 devices: a whole 4x4x4 slice. The times are simulated.
128 devices in a mesh: sx: 16 (over z, y), sy: 8 (over x, core).
Axes of the slice: x: 4, y: 4, z: 4, core: 2. Of those that a mesh axis runs over, the one named last changes fastest.
Arguments:
- obs_values: bfloat16 [32768, 64], P(('sx', 'sy')), may hold values from -6 to 6
- obs_dest: int32 [32768, 1], P(('sx', 'sy')), may hold values from 0 to 127; in each aligned block of 256 rows (0 to 255, 256 to 511, ...) at most 4 rows name the same one
- obs_node: int32 [32768], P(('sx', 'sy')), may hold values from 0 to 2047
- schur: bfloat16 [16, 8, 2048, 2048], P('sx', 'sy'), as said below
- local_inverse: bfloat16 [16, 8, 2048, 2048], P('sx', 'sy'), as said below
- coarse_inverse: float32 [1024, 1024], P(('sx', 'sy')), as said below
Outputs:
- solution_field: float32 [16, 8, 64, 2048], P('sx', 'sy')
- residual: float32 [16, 8, 64, 2048], P('sx', 'sy')
Inputs may be any that keep to these rules, and one draw needn't show every extreme that they name: `obs_dest`: at most 4 observations of one device go to one subdomain. `schur`: symmetric positive definite. `local_inverse`: symmetric positive definite. `coarse_inverse`: symmetric positive definite.
All inputs are finite; a program needn't handle non-finite values.
Results may differ from a plain program's by a relative error of at most 0.04.
Values may be sent and summed in bfloat16 or wider, within the bound.
A program may use at most 128 MiB of HBM per device.

v0:
```python
import jax
import jax.numpy as jnp
from jax import lax
from jax.sharding import PartitionSpec as P

ITERS = 6


def shortened(array):

    def short(part):
        return part.astype(jnp.bfloat16) if part.dtype == jnp.float32 else part

    return jax.tree.map(short, array)


def padded_2(cells, sides, width):
    for axis, dim in sides:
        count = lax.axis_size(axis)
        ends = count - 1
        head = lax.slice_in_dim(cells, 0, width, axis=dim)
        tail = lax.slice_in_dim(cells, cells.shape[dim] - width, cells.shape[dim], axis=dim)
        cells = jnp.concatenate(
            [
                lax.ppermute(tail, axis, [(i, (i + 1) % count) for i in range(ends)]),
                cells,
                lax.ppermute(head, axis, [((i + 1) % count, i) for i in range(ends)]),
            ],
            axis=dim,
        )
    return cells


def edge_weights(size):
    edge_len = size // 4
    col_index = lax.axis_index("sx")
    row_index = lax.axis_index("sy")
    col_count = lax.axis_size("sx")
    row_count = lax.axis_size("sy")
    sides = (
        jnp.where(col_index > 0, 0.5, 1.0),
        jnp.where(col_index < col_count - 1, 0.5, 1.0),
        jnp.where(row_index > 0, 0.5, 1.0),
        jnp.where(row_index < row_count - 1, 0.5, 1.0),
    )
    return jnp.concatenate([jnp.full((edge_len,), value, jnp.float32) for value in sides])


def coarse_basis(size, count):
    edge_len = size // 4
    node = jnp.arange(size)
    side = node // edge_len
    offset = (node % edge_len).astype(jnp.float32) - (edge_len - 1) / 2.0
    norm_ramp = jnp.sqrt(jnp.float32(edge_len * (edge_len * edge_len - 1) / 12.0))
    column = jnp.arange(count)
    on_edge = side[:, None] == (column // 2)[None, :]
    value = jnp.where(
        (column % 2 == 0)[None, :],
        1.0 / jnp.sqrt(jnp.float32(edge_len)),
        offset[:, None] / norm_ramp,
    )
    return jnp.where(on_edge, value, 0.0)


def assemble(local):
    edge_len = local.shape[1] // 4
    west_part = local[:, 0:edge_len]
    east_part = local[:, edge_len : 2 * edge_len]
    south_part = local[:, 2 * edge_len : 3 * edge_len]
    north_part = local[:, 3 * edge_len :]
    padded = padded_2(shortened(local[None, None]), (("sx", 0), ("sy", 1)), 1)
    west = west_part + padded[0, 1, :, edge_len : 2 * edge_len]
    east = east_part + padded[2, 1, :, 0:edge_len]
    south = south_part + padded[1, 0, :, 3 * edge_len :]
    north = north_part + padded[1, 2, :, 2 * edge_len : 3 * edge_len]
    return jnp.concatenate([west, east, south, north], axis=1)


def gather_coarse(coarse_local):
    return lax.all_gather(coarse_local, ("sx", "sy"), axis=0, tiled=True)


def body(obs_values, obs_dest, obs_node, schur, local_inverse, coarse_inverse):
    hp = lax.Precision.HIGHEST
    size = schur.shape[-1]
    count = coarse_inverse.shape[0]
    realiz = obs_values.shape[1]
    obs_count = obs_values.shape[0]
    row_count = lax.axis_size("sy")
    dev_count = lax.axis_size("sx") * row_count
    target = obs_dest[:, 0]
    capacity = max(2, 2 * obs_count // dev_count)
    match_table = (target[:, None] == jnp.arange(dev_count)[None, :]).astype(jnp.int32)
    slot_index = jnp.sum(jnp.cumsum(match_table, axis=0) * match_table, axis=1) - 1
    position = target * capacity + slot_index
    send_values = (
        jnp.zeros((dev_count * capacity, realiz), jnp.bfloat16).at[position].set(obs_values)
    )
    send_nodes = jnp.zeros((dev_count * capacity,), jnp.int32).at[position].set(obs_node)
    got_values, got_nodes = (
        lax.all_to_all(
            send_values.reshape(dev_count, capacity, realiz),
            ("sx", "sy"),
            split_axis=0,
            concat_axis=0,
            tiled=True,
        ),
        lax.all_to_all(
            send_nodes.reshape(dev_count, capacity),
            ("sx", "sy"),
            split_axis=0,
            concat_axis=0,
            tiled=True,
        ),
    )
    load = jax.ops.segment_sum(
        got_values.reshape(-1, realiz).astype(jnp.float32), got_nodes.reshape(-1), num_segments=size
    )
    rhs = assemble(load.T)
    weight = edge_weights(size)[None, :]
    basis = coarse_basis(size, count)
    schur_mat = schur[0, 0]
    inverse_mat = local_inverse[0, 0]

    def project(vec):
        return jnp.dot(weight * vec, basis, precision=hp).T

    def precond(vec, coarse_all):
        scaled = weight * vec
        part = jnp.dot(scaled.astype(jnp.bfloat16), inverse_mat, preferred_element_type=jnp.float32)
        solved = jnp.dot(coarse_inverse, coarse_all, precision=hp)
        correction = jnp.dot(solved.T, basis.T, precision=hp)
        return assemble(weight * (part + correction))

    def products(left, right):
        return lax.psum(jnp.sum(weight * left * right, axis=1), ("sx", "sy"))

    solution_field = jnp.zeros_like(rhs)
    residual = rhs
    coarse_resid = gather_coarse(project(residual))
    precon = precond(residual, coarse_resid)
    direction = precon
    rz_now = products(residual, precon)
    for step in range(ITERS):
        image = assemble(
            jnp.dot(direction.astype(jnp.bfloat16), schur_mat, preferred_element_type=jnp.float32)
        )
        curv_local = jnp.sum(weight * direction * image, axis=1)
        curv = lax.psum(curv_local, ("sx", "sy"))
        alpha = rz_now / curv
        solution_field = solution_field + alpha[:, None] * direction
        residual = residual - alpha[:, None] * image
        if step < ITERS - 1:
            coarse_resid = gather_coarse(project(residual))
            precon = precond(residual, coarse_resid)
            rz_next = products(residual, precon)
            direction = precon + (rz_next / rz_now)[:, None] * direction
            rz_now = rz_next
    return (solution_field[None, None], residual[None, None])


def solution(mesh):
    placed = (
        P(("sx", "sy"), None),
        P(("sx", "sy"), None),
        P(("sx", "sy")),
        P("sx", "sy", None, None),
        P("sx", "sy", None, None),
        P(("sx", "sy"), None),
    )
    return jax.shard_map(
        body,
        mesh=mesh,
        in_specs=placed,
        out_specs=(P("sx", "sy", None, None), P("sx", "sy", None, None)),
        check_vma=False,
    )
```

profile of v0, /device:TPU:1, one launch (start us, length us, event | category | flops | bytes accessed | tf_op | source)
XLA Modules:
  0.0 1432.0 jit_solution(6117860953516433841)
XLA Ops:
  5.6 11.5 all-to-all-start
  19.9 6.7 all-to-all-done
  26.6 4.5 all-to-all-start.1
  32.6 8.1 all-to-all-done.1
  45.1 4.0 collective-permute-start
  60.7 7.6 collective-permute-done.3
  72.7 39.9 %all_gather.18 = f32[1024,64]{1,0:T(8,128)S(1)} all-gather(f32[8,64]{1,0:T(8,128)S(1)} %fusion.35), channel_id=1, replica_groups=mesh['sx'=16,'sy'=8] {'sx','sy'}, dimensions={0}, use_global_device_ids=true | all-gather | bytes 264192 | tf_op jit(solution)/shard_map/all_gather | solution.py:80
  112.6 5.1 fusion.22
  125.1 4.3 collective-permute-done.5
  136.0 7.7 collective-permute-done.7
  147.9 4.8 collective-permute-start.8
  158.0 5.3 collective-permute-start.10
  163.3 7.7 collective-permute-done.11
  172.5 69.8 %all-reduce = (f32[64]{0:T(128)S(1)}, f32[64]{0:T(128)S(1)}) all-reduce(f32[64]{0:T(128)S(1)} %get-tuple-element.3, f32[64]{0:T(128)S(1)} %get-tuple-element.2), channel_id=1, replica_groups=mesh['sx'=16,'sy'=8] {'sx','sy'}, use_global_device_ids=true, to_apply=%region_7.8 | all-reduce | flops 128 | bytes 1024 | tf_op jit(solution)/shard_map/psum | solution.py:136
  244.8 5.0 fusion.20
  249.8 34.5 %all_gather.19 = f32[1024,64]{1,0:T(8,128)S(1)} all-gather(f32[8,64]{1,0:T(8,128)S(1)} %fusion.34), channel_id=1, replica_groups=mesh['sx'=16,'sy'=8] {'sx','sy'}, dimensions={0}, use_global_device_ids=true | all-gather | bytes 264192 | tf_op jit(solution)/shard_map/all_gather | solution.py:80
  287.7 4.0 collective-permute-start.12
  291.7 4.3 collective-permute-done.13
  302.5 7.7 collective-permute-done.15
  311.7 67.8 %psum.86 = f32[64]{0:T(128)S(1)} all-reduce(f32[64]{0:T(128)S(1)} %multiply_reduce_fusion.8), channel_id=1, replica_groups=mesh['sx'=16,'sy'=8] {'sx','sy'}, use_global_device_ids=true, to_apply=%region_11.12 | all-reduce | flops 64 | bytes 512 | tf_op jit(solution)/shard_map/psum | solution.py:136
  379.7 4.9 fusion.8
  394.3 4.2 collective-permute-start.19
  400.4 7.4 collective-permute-done.19
  409.6 68.1 %psum.87 = f32[64]{0:T(128)S(1)} all-reduce(f32[64]{0:T(128)S(1)} %multiply_reduce_fusion.7), channel_id=1, replica_groups=mesh['sx'=16,'sy'=8] {'sx','sy'}, use_global_device_ids=true, to_apply=%region_13.14 | all-reduce | flops 64 | bytes 512 | tf_op jit(solution)/shard_map/psum | solution.py:149
  480.2 4.9 fusion.18
  485.2 34.6 %all_gather.20 = f32[1024,64]{1,0:T(8,128)S(1)} all-gather(f32[8,64]{1,0:T(8,128)S(1)} %fusion.33), channel_id=1, replica_groups=mesh['sx'=16,'sy'=8] {'sx','sy'}, dimensions={0}, use_global_device_ids=true | all-gather | bytes 264192 | tf_op jit(solution)/shard_map/all_gather | solution.py:80
  523.1 4.0 collective-permute-start.20
  527.1 4.3 collective-permute-done.21
  538.0 7.7 collective-permute-done.23
  547.9 68.0 %psum.88 = f32[64]{0:T(128)S(1)} all-reduce(f32[64]{0:T(128)S(1)} %multiply_reduce_fusion.6), channel_id=1, replica_groups=mesh['sx'=16,'sy'=8] {'sx','sy'}, use_global_device_ids=true, to_apply=%region_15.16 | all-reduce | flops 64 | bytes 512 | tf_op jit(solution)/shard_map/psum | solution.py:136
  617.1 4.9 fusion.6
  623.4 4.0 collective-permute-start.24
  631.7 4.2 collective-permute-start.27
  637.8 7.3 collective-permute-done.27
  647.0 68.1 %psum.89 = f32[64]{0:T(128)S(1)} all-reduce(f32[64]{0:T(128)S(1)} %multiply_reduce_fusion.5), channel_id=1, replica_groups=mesh['sx'=16,'sy'=8] {'sx','sy'}, use_global_device_ids=true, to_apply=%region_17.18 | all-reduce | flops 64 | bytes 512 | tf_op jit(solution)/shard_map/psum | solution.py:149
  718.6 5.0 fusion.16
  723.6 34.8 %all_gather.21 = f32[1024,64]{1,0:T(8,128)S(1)} all-gather(f32[8,64]{1,0:T(8,128)S(1)} %fusion.32), channel_id=1, replica_groups=mesh['sx'=16,'sy'=8] {'sx','sy'}, dimensions={0}, use_global_device_ids=true | all-gather | bytes 264192 | tf_op jit(solution)/shard_map/all_gather | solution.py:80
  765.7 4.3 collective-permute-done.29
  776.6 7.7 collective-permute-done.31
  785.8 68.0 %psum.90 = f32[64]{0:T(128)S(1)} all-reduce(f32[64]{0:T(128)S(1)} %multiply_reduce_fusion.4), channel_id=1, replica_groups=mesh['sx'=16,'sy'=8] {'sx','sy'}, use_global_device_ids=true, to_apply=%region_19.20 | all-reduce | flops 64 | bytes 512 | tf_op jit(solution)/shard_map/psum | solution.py:136
  854.0 4.9 fusion.4
  868.5 4.2 collective-permute-start.35
  874.7 7.3 collective-permute-done.35
  883.9 68.1 %psum.91 = f32[64]{0:T(128)S(1)} all-reduce(f32[64]{0:T(128)S(1)} %multiply_reduce_fusion.3), channel_id=1, replica_groups=mesh['sx'=16,'sy'=8] {'sx','sy'}, use_global_device_ids=true, to_apply=%region_21.22 | all-reduce | flops 64 | bytes 512 | tf_op jit(solution)/shard_map/psum | solution.py:149
  954.4 5.0 fusion.14
  959.4 34.5 %all_gather.22 = f32[1024,64]{1,0:T(8,128)S(1)} all-gather(f32[8,64]{1,0:T(8,128)S(1)} %fusion.31), channel_id=1, replica_groups=mesh['sx'=16,'sy'=8] {'sx','sy'}, dimensions={0}, use_global_device_ids=true | all-gather | bytes 264192 | tf_op jit(solution)/shard_map/all_gather | solution.py:80
  997.3 4.0 collective-permute-start.36
  1001.3 4.3 collective-permute-done.37
  1012.2 7.7 collective-permute-done.39
  1022.2 68.0 %psum.92 = f32[64]{0:T(128)S(1)} all-reduce(f32[64]{0:T(128)S(1)} %multiply_reduce_fusion.2), channel_id=1, replica_groups=mesh['sx'=16,'sy'=8] {'sx','sy'}, use_global_device_ids=true, to_apply=%region_23.24 | all-reduce | flops 64 | bytes 512 | tf_op jit(solution)/shard_map/psum | solution.py:136
  1091.4 4.9 fusion.2
  1106.0 4.2 collective-permute-start.43
  1112.1 7.3 collective-permute-done.43
  1121.3 68.1 %psum.93 = f32[64]{0:T(128)S(1)} all-reduce(f32[64]{0:T(128)S(1)} %multiply_reduce_fusion.1), channel_id=1, replica_groups=mesh['sx'=16,'sy'=8] {'sx','sy'}, use_global_device_ids=true, to_apply=%region_25.26 | all-reduce | flops 64 | bytes 512 | tf_op jit(solution)/shard_map/psum | solution.py:149
  1191.8 5.0 fusion.12
  1196.8 34.6 %all_gather.23 = f32[1024,64]{1,0:T(8,128)S(1)} all-gather(f32[8,64]{1,0:T(8,128)S(1)} %fusion.30), channel_id=1, replica_groups=mesh['sx'=16,'sy'=8] {'sx','sy'}, dimensions={0}, use_global_device_ids=true | all-gather | bytes 264192 | tf_op jit(solution)/shard_map/all_gather | solution.py:80
  1234.7 4.0 collective-permute-start.44
  1238.8 4.3 collective-permute-done.45
  1249.6 7.7 collective-permute-done.47
  1258.8 68.0 %psum.94 = f32[64]{0:T(128)S(1)} all-reduce(f32[64]{0:T(128)S(1)} %multiply_reduce_fusion), channel_id=1, replica_groups=mesh['sx'=16,'sy'=8] {'sx','sy'}, use_global_device_ids=true, to_apply=%region_27.28 | all-reduce | flops 64 | bytes 512 | tf_op jit(solution)/shard_map/psum | solution.py:136
  1326.8 5.0 fusion
  1341.5 4.2 collective-permute-start.51
  1347.6 7.3 collective-permute-done.51
  1357.7 68.1 %psum.95 = f32[64]{0:T(128)S(1)} all-reduce(f32[64]{0:T(128)S(1)} %fusion.48), channel_id=1, replica_groups=mesh['sx'=16,'sy'=8] {'sx','sy'}, use_global_device_ids=true, to_apply=%region_29.30 | all-reduce | flops 64 | bytes 512 | tf_op jit(solution)/shard_map/psum | solution.py:149
  (284 shorter events, 201.6 us)
Async XLA Ops:
  0.6 117.1 %copy-start = (f32[8,1024]{1,0:T(8,128)S(1)}, f32[8,1024]{1,0:T(8,128)}, u32[]{:S(2)}) copy-start(f32[8,1024]{1,0:T(8,128)} %param.11) | copy-start | bytes 98308
  5.6 21.0 %all-to-all-start = ((s32[128,1,4]{2,1,0:T(1,128)}), s32[128,1,4]{2,1,0:T(1,128)S(1)}, u32[]{:S(2)}, u32[]{:S(2)}) async-start(s32[128,1,4]{2,1,0:T(1,128)} %bitcast.7), calls=%async_computation | async-start | bytes 131072 | tf_op jit(solution)/shard_map/all_to_all | solution.py:108
  26.6 14.0 all-to-all-start.1
  43.8 9.0 collective-permute-start.1
  45.1 8.5 collective-permute-start
  53.7 14.6 %collective-permute-start.3 = (bf16[3,1,64,2048]{3,2,1,0:T(8,128)(2,1)S(1)}, bf16[3,1,64,2048]{3,2,1,0:T(8,128)(2,1)S(1)}, u32[]{:S(2)}, u32[]{:S(2)}) collective-permute-start(bf16[3,1,64,2048]{3,2,1,0:T(8,128)(2,1)S(1)} %pad_maximum_fusion), channel_id=1, source_target_pairs={{1,0},{2,1},{3,2},{4,3},{5,4},{6,5},{7,6},{9,8},{10,9},{11,10},{12... | collective-permute-start | bytes 2359304 | tf_op jit(solution)/shard_map/ppermute | solution.py:27
  57.6 11.9 collective-permute-start.2
  119.8 9.6 collective-permute-start.5
  121.1 9.2 collective-permute-start.4
  130.4 13.3 collective-permute-start.7
  133.6 11.3 collective-permute-start.6
  146.6 7.9 collective-permute-start.9
  147.9 8.0 collective-permute-start.8
  156.1 15.0 %collective-permute-start.11 = (bf16[3,1,64,2048]{3,2,1,0:T(8,128)(2,1)S(1)}, bf16[3,1,64,2048]{3,2,1,0:T(8,128)(2,1)S(1)}, u32[]{:S(2)}, u32[]{:S(2)}) collective-permute-start(bf16[3,1,64,2048]{3,2,1,0:T(8,128)(2,1)S(1)} %pad_maximum_fusion.2), channel_id=1, source_target_pairs={{1,0},{2,1},{3,2},{4,3},{5,4},{6,5},{7,6},{9,8},{10,9},{11,10},{12... | collective-permute-start | bytes 2359304 | tf_op jit(solution)/shard_map/ppermute | solution.py:27
  158.0 14.2 collective-permute-start.10
  286.4 9.6 collective-permute-start.13
  287.7 9.2 collective-permute-start.12
  297.0 13.3 collective-permute-start.15
  300.2 11.3 collective-permute-start.14
  384.7 8.6 collective-permute-start.17
  386.0 8.2 collective-permute-start.16
  394.3 13.5 collective-permute-start.19
  398.5 10.8 collective-permute-start.18
  521.8 9.6 collective-permute-start.21
  523.1 9.2 collective-permute-start.20
  532.4 13.3 collective-permute-start.23
  535.6 11.3 collective-permute-start.22
  622.1 8.6 collective-permute-start.25
  623.4 8.2 collective-permute-start.24
  631.7 13.4 collective-permute-start.27
  635.9 10.8 collective-permute-start.26
  760.4 9.6 collective-permute-start.29
  761.7 9.2 collective-permute-start.28
  771.0 13.3 collective-permute-start.31
  774.2 11.3 collective-permute-start.30
  858.9 8.6 collective-permute-start.33
  860.2 8.2 collective-permute-start.32
  868.5 13.4 collective-permute-start.35
  872.8 10.8 collective-permute-start.34
  883.7 75.7 %copy-start.27 = (f32[64,512]{1,0:T(8,128)}, f32[64,512]{1,0:T(8,128)S(1)}, u32[]{:S(2)}) copy-start(f32[64,512]{1,0:T(8,128)S(1)} %get-tuple-element.22) | copy-start | bytes 393220
  996.0 9.6 collective-permute-start.37
  997.3 9.2 collective-permute-start.36
  1006.6 13.3 collective-permute-start.39
  1009.8 11.3 collective-permute-start.38
  1096.4 8.6 collective-permute-start.41
  1097.7 8.2 collective-permute-start.40
  1106.0 13.4 collective-permute-start.43
  1110.2 10.8 collective-permute-start.42
  1121.1 75.7 %copy-start.35 = (f32[64,512]{1,0:T(8,128)}, f32[64,512]{1,0:T(8,128)S(1)}, u32[]{:S(2)}) copy-start(f32[64,512]{1,0:T(8,128)S(1)} %get-tuple-element.14) | copy-start | bytes 393220
  1121.1 75.7 %copy-start.36 = (f32[64,512]{1,0:T(8,128)}, f32[64,512]{1,0:T(8,128)S(1)}, u32[]{:S(2)}) copy-start(f32[64,512]{1,0:T(8,128)S(1)} %get-tuple-element.15) | copy-start | bytes 393220
  1121.1 75.7 %copy-start.37 = (f32[64,512]{1,0:T(8,128)}, f32[64,512]{1,0:T(8,128)S(1)}, u32[]{:S(2)}) copy-start(f32[64,512]{1,0:T(8,128)S(1)} %get-tuple-element.16) | copy-start | bytes 393220
  1121.1 75.7 %copy-start.38 = (f32[64,512]{1,0:T(8,128)}, f32[64,512]{1,0:T(8,128)S(1)}, u32[]{:S(2)}) copy-start(f32[64,512]{1,0:T(8,128)S(1)} %get-tuple-element.17) | copy-start | bytes 393220
  1233.4 9.6 collective-permute-start.45
  1234.7 9.2 collective-permute-start.44
  1244.0 13.3 collective-permute-start.47
  1247.2 11.3 collective-permute-start.46
  1258.6 167.2 %copy-start.6 = (f32[64,512]{1,0:T(8,128)S(1)}, f32[64,512]{1,0:T(8,128)}, u32[]{:S(2)}) copy-start(f32[64,512]{1,0:T(8,128)} %copy-done.5) | copy-start | bytes 393220
  1258.6 167.2 %copy-start.8 = (f32[64,512]{1,0:T(8,128)S(1)}, f32[64,512]{1,0:T(8,128)}, u32[]{:S(2)}) copy-start(f32[64,512]{1,0:T(8,128)} %copy-done.7) | copy-start | bytes 393220
  1326.8 101.9 %copy-start.2 = (f32[64,512]{1,0:T(8,128)S(1)}, f32[64,512]{1,0:T(8,128)}, u32[]{:S(2)}) copy-start(f32[64,512]{1,0:T(8,128)} %copy-done.1) | copy-start | bytes 393220
  1326.8 101.9 %copy-start.4 = (f32[64,512]{1,0:T(8,128)S(1)}, f32[64,512]{1,0:T(8,128)}, u32[]{:S(2)}) copy-start(f32[64,512]{1,0:T(8,128)} %copy-done.3) | copy-start | bytes 393220
  1331.9 8.6 collective-permute-start.49
  1333.2 8.2 collective-permute-start.48
  1341.5 13.5 collective-permute-start.51
  1345.7 10.8 collective-permute-start.50
  (35 other events, 1586.3 us)
where the time goes:
time: 1440 us; the launch traced here: 1430 us
  blocking collectives  963 us (67%)
  waiting for transfers between devices  190 us (13%)
  starting transfers between devices  164 us (11%)
  matrix products  82.1 us (6%)
  other arithmetic  20.9 us (1%)
    psum x6, blocking collectives, products(): return lax.psum(jnp.sum(weight * left * right, axis=1), ('sx', 'sy'))  410 us
    psum x5, blocking collectives, body(): curv = lax.psum(curv_local, ('sx', 'sy'))  340 us
    all_gather x6, blocking collectives, gather_coarse(): return lax.all_gather(coarse_local, ('sx', 'sy'), axis=0, tiled=True)  213 us
    ppermute x26, waiting for transfers between devices, padded_2(): lax.ppermute(head, axis, [((i + 1) % count, i) for i in range(ends)])  146 us
    ppermute x26, starting transfers between devices, padded_2(): lax.ppermute(tail, axis, [(i, (i + 1) % count) for i in range(ends)])  84.9 us
    ppermute x26, starting transfers between devices, padded_2(): lax.ppermute(head, axis, [((i + 1) % count, i) for i in range(ends)])  62.8 us
    dot_general x6, matrix products, precond(): jnp.dot(scaled.astype(jnp.bfloat16), inverse_mat, preferred_element_type=...  29.9 us
    ppermute x26, waiting for transfers between devices, padded_2(): lax.ppermute(tail, axis, [(i, (i + 1) % count) for i in range(ends)])  29.5 us
  transfers between devices with their start and end apart: 54, of which 54 were waited for; matrix products, arithmetic and copies ran while one was open for 0% of the time, Pallas kernels for 0%

commit v1 on v0

--- a/solution.py
+++ b/solution.py
@@ -77,7 +77,10 @@
 
 
 def gather_coarse(coarse_local):
-    return lax.all_gather(coarse_local, ("sx", "sy"), axis=0, tiled=True)
+    return jnp.concatenate(
+        lax.all_to_all(jnp.stack([coarse_local] * lax.axis_size(("sx", "sy"))), ("sx", "sy"), 0, 0),
+        axis=0,
+    )
 
 
 def body(obs_values, obs_dest, obs_node, schur, local_inverse, coarse_inverse):

time: 1440 us -> 1320 us (0.917)
  blocking collectives: 963 us -> 745 us
  starting transfers between devices: 164 us -> 205 us
  waiting for transfers between devices: 190 us -> 219 us
    all_gather x6 -> x0, blocking collectives: 213 us -> none  [gather_coarse(): return lax.all_gather(coarse_local, ('sx', 'sy'), axis=0, tiled=True)]
    all_to_all x0 -> x6, starting transfers between devices: none -> 39.6 us  [gather_coarse(): lax.all_to_all(jnp.stack([coarse_local] * lax.axis_size(('sx', 'sy'))), (...]
    all_to_all x0 -> x6, waiting for transfers between devices: none -> 32.4 us  [gather_coarse(): lax.all_to_all(jnp.stack([coarse_local] * lax.axis_size(('sx', 'sy'))), (...]
  transfers between devices with their start and end apart: 54 -> 60, of which waited for: 54 -> 60; matrix products, arithmetic and copies ran while one was open for 0% -> 3% of each run, Pallas kernels for 0% -> 0%
where the time goes in v1:
time: 1320 us; the launch traced here: 1310 us
  blocking collectives  745 us (56%)
  waiting for transfers between devices  219 us (17%)
  starting transfers between devices  205 us (16%)
  matrix products  94 us (7%)
  other arithmetic  28.3 us (2%)
  local copies, waits for them, and re-layouts  17.3 us (1%)
    psum x6, blocking collectives, products(): return lax.psum(jnp.sum(weight * left * right, axis=1), ('sx', 'sy'))  405 us
    psum x5, blocking collectives, body(): curv = lax.psum(curv_local, ('sx', 'sy'))  339 us
    ppermute x26, waiting for transfers between devices, padded_2(): lax.ppermute(head, axis, [((i + 1) % count, i) for i in range(ends)])  145 us
    ppermute x26, starting transfers between devices, padded_2(): lax.ppermute(tail, axis, [(i, (i + 1) % count) for i in range(ends)])  83.7 us
    ppermute x26, starting transfers between devices, padded_2(): lax.ppermute(head, axis, [((i + 1) % count, i) for i in range(ends)])  66.2 us
    all_to_all x6, starting transfers between devices, gather_coarse(): lax.all_to_all(jnp.stack([coarse_local] * lax.axis_size(('sx', 'sy'))), (...  39.6 us
    dot_general x6, matrix products, precond(): jnp.dot(scaled.astype(jnp.bfloat16), inverse_mat, preferred_element_type=...  32.9 us
    all_to_all x6, waiting for transfers between devices, gather_coarse(): lax.all_to_all(jnp.stack([coarse_local] * lax.axis_size(('sx', 'sy'))), (...  32.4 us
  transfers between devices with their start and end apart: 60, of which 60 were waited for; matrix products, arithmetic and copies ran while one was open for 3% of the time, Pallas kernels for 0%

profile of v1, /device:TPU:1, one launch (start us, length us, event | category | flops | bytes accessed | tf_op | source)
XLA Modules:
  0.0 1312.0 jit_solution(12134029944559749624)
XLA Ops:
  5.6 11.5 all-to-all-start
  19.9 6.7 all-to-all-done
  26.6 4.5 all-to-all-start.1
  32.6 8.1 all-to-all-done.1
  45.1 4.0 collective-permute-start
  60.7 7.6 collective-permute-done.3
  73.8 11.2 all-to-all-start.2
  85.1 5.0 fusion.22
  90.0 5.9 all-to-all-done.2
  101.3 4.0 collective-permute-start.4
  115.9 7.7 collective-permute-done.7
  124.9 5.0 fusion.10
  131.2 4.8 collective-permute-start.8
  141.2 5.6 collective-permute-start.10
  146.8 7.7 collective-permute-done.11
  156.1 69.0 %all-reduce = (f32[64]{0:T(128)S(1)}, f32[64]{0:T(128)S(1)}) all-reduce(f32[64]{0:T(128)S(1)} %get-tuple-element.3, f32[64]{0:T(128)S(1)} %get-tuple-element.2), channel_id=1, replica_groups=mesh['sx'=16,'sy'=8] {'sx','sy'}, use_global_device_ids=true, to_apply=%region_7.8 | all-reduce | flops 128 | bytes 1024 | tf_op jit(solution)/shard_map/psum | solution.py:139
  228.6 5.5 all-to-all-start.3
  234.1 4.9 fusion.20
  239.1 5.9 all-to-all-done.3
  249.7 4.0 collective-permute-start.12
  264.3 7.7 collective-permute-done.15
  273.5 67.2 %psum.86 = f32[64]{0:T(128)S(1)} all-reduce(f32[64]{0:T(128)S(1)} %multiply_reduce_fusion.8), channel_id=1, replica_groups=mesh['sx'=16,'sy'=8] {'sx','sy'}, use_global_device_ids=true, to_apply=%region_11.12 | all-reduce | flops 64 | bytes 512 | tf_op jit(solution)/shard_map/psum | solution.py:139
  340.9 4.9 fusion.8
  347.2 4.0 collective-permute-start.16
  361.6 7.7 collective-permute-done.19
  370.8 68.0 %psum.87 = f32[64]{0:T(128)S(1)} all-reduce(f32[64]{0:T(128)S(1)} %multiply_reduce_fusion.7), channel_id=1, replica_groups=mesh['sx'=16,'sy'=8] {'sx','sy'}, use_global_device_ids=true, to_apply=%region_13.14 | all-reduce | flops 64 | bytes 512 | tf_op jit(solution)/shard_map/psum | solution.py:152
  442.3 5.6 all-to-all-start.4
  447.9 5.7 fusion.18
  453.7 5.1 all-to-all-done.4
  464.9 4.0 collective-permute-start.20
  479.5 7.7 collective-permute-done.23
  489.5 67.4 %psum.88 = f32[64]{0:T(128)S(1)} all-reduce(f32[64]{0:T(128)S(1)} %multiply_reduce_fusion.6), channel_id=1, replica_groups=mesh['sx'=16,'sy'=8] {'sx','sy'}, use_global_device_ids=true, to_apply=%region_15.16 | all-reduce | flops 64 | bytes 512 | tf_op jit(solution)/shard_map/psum | solution.py:139
  558.1 4.9 fusion.6
  564.4 4.0 collective-permute-start.24
  572.7 4.2 collective-permute-start.27
  578.8 7.6 collective-permute-done.27
  588.0 67.8 %psum.89 = f32[64]{0:T(128)S(1)} all-reduce(f32[64]{0:T(128)S(1)} %multiply_reduce_fusion.5), channel_id=1, replica_groups=mesh['sx'=16,'sy'=8] {'sx','sy'}, use_global_device_ids=true, to_apply=%region_17.18 | all-reduce | flops 64 | bytes 512 | tf_op jit(solution)/shard_map/psum | solution.py:152
  660.5 6.0 all-to-all-start.5
  666.5 5.7 fusion.16
  672.3 5.1 all-to-all-done.5
  683.5 4.0 collective-permute-start.28
  698.2 7.7 collective-permute-done.31
  707.3 67.3 %psum.90 = f32[64]{0:T(128)S(1)} all-reduce(f32[64]{0:T(128)S(1)} %multiply_reduce_fusion.4), channel_id=1, replica_groups=mesh['sx'=16,'sy'=8] {'sx','sy'}, use_global_device_ids=true, to_apply=%region_19.20 | all-reduce | flops 64 | bytes 512 | tf_op jit(solution)/shard_map/psum | solution.py:139
  774.8 4.9 fusion.4
  781.1 4.0 collective-permute-start.32
  795.5 7.7 collective-permute-done.35
  804.7 67.9 %psum.91 = f32[64]{0:T(128)S(1)} all-reduce(f32[64]{0:T(128)S(1)} %multiply_reduce_fusion.3), channel_id=1, replica_groups=mesh['sx'=16,'sy'=8] {'sx','sy'}, use_global_device_ids=true, to_apply=%region_21.22 | all-reduce | flops 64 | bytes 512 | tf_op jit(solution)/shard_map/psum | solution.py:152
  876.2 5.6 all-to-all-start.6
  881.8 5.7 fusion.14
  887.5 5.1 all-to-all-done.6
  913.4 7.7 collective-permute-done.39
  923.4 67.3 %psum.92 = f32[64]{0:T(128)S(1)} all-reduce(f32[64]{0:T(128)S(1)} %multiply_reduce_fusion.2), channel_id=1, replica_groups=mesh['sx'=16,'sy'=8] {'sx','sy'}, use_global_device_ids=true, to_apply=%region_23.24 | all-reduce | flops 64 | bytes 512 | tf_op jit(solution)/shard_map/psum | solution.py:139
  991.9 4.9 fusion.2
  1012.7 7.7 collective-permute-done.43
  1021.9 67.8 %psum.93 = f32[64]{0:T(128)S(1)} all-reduce(f32[64]{0:T(128)S(1)} %multiply_reduce_fusion.1), channel_id=1, replica_groups=mesh['sx'=16,'sy'=8] {'sx','sy'}, use_global_device_ids=true, to_apply=%region_25.26 | all-reduce | flops 64 | bytes 512 | tf_op jit(solution)/shard_map/psum | solution.py:152
  1093.2 5.7 all-to-all-start.7
  1098.9 5.7 fusion.12
  1104.7 5.1 all-to-all-done.7
  1130.5 7.7 collective-permute-done.47
  1139.7 67.4 %psum.94 = f32[64]{0:T(128)S(1)} all-reduce(f32[64]{0:T(128)S(1)} %multiply_reduce_fusion), channel_id=1, replica_groups=mesh['sx'=16,'sy'=8] {'sx','sy'}, use_global_device_ids=true, to_apply=%region_27.28 | all-reduce | flops 64 | bytes 512 | tf_op jit(solution)/shard_map/psum | solution.py:139
  1207.0 5.0 fusion
  1221.7 4.2 collective-permute-start.51
  1227.9 7.6 collective-permute-done.51
  1237.9 67.8 %psum.95 = f32[64]{0:T(128)S(1)} all-reduce(f32[64]{0:T(128)S(1)} %fusion.48), channel_id=1, replica_groups=mesh['sx'=16,'sy'=8] {'sx','sy'}, use_global_device_ids=true, to_apply=%region_29.30 | all-reduce | flops 64 | bytes 512 | tf_op jit(solution)/shard_map/psum | solution.py:152
  (310 shorter events, 248.3 us)
Async XLA Ops:
  5.6 21.0 %all-to-all-start = ((s32[128,1,4]{2,1,0:T(1,128)}), s32[128,1,4]{2,1,0:T(1,128)S(1)}, u32[]{:S(2)}, u32[]{:S(2)}) async-start(s32[128,1,4]{2,1,0:T(1,128)} %bitcast.7), calls=%async_computation | async-start | bytes 131072 | tf_op jit(solution)/shard_map/all_to_all | solution.py:111
  26.6 14.0 %all-to-all-start.1 = ((bf16[128,2,128]{2,1,0:T(2,128)(2,1)}), bf16[128,2,128]{2,1,0:T(2,128)(2,1)S(1)}, u32[]{:S(2)}, u32[]{:S(2)}) async-start(bf16[128,2,128]{2,1,0:T(2,128)(2,1)} %reshape.1450), calls=%async_computation.1 | async-start | bytes 131072 | tf_op jit(solution)/shard_map/all_to_all | solution.py:104
  43.8 9.0 collective-permute-start.1
  45.1 8.5 collective-permute-start
  53.7 14.6 %collective-permute-start.3 = (bf16[3,1,64,2048]{3,2,1,0:T(8,128)(2,1)S(1)}, bf16[3,1,64,2048]{3,2,1,0:T(8,128)(2,1)S(1)}, u32[]{:S(2)}, u32[]{:S(2)}) collective-permute-start(bf16[3,1,64,2048]{3,2,1,0:T(8,128)(2,1)S(1)} %pad_maximum_fusion), channel_id=1, source_target_pairs={{1,0},{2,1},{3,2},{4,3},{5,4},{6,5},{7,6},{9,8},{10,9},{11,10},{12... | collective-permute-start | bytes 2359304 | tf_op jit(solution)/shard_map/ppermute | solution.py:27
  57.6 11.9 collective-permute-start.2
  73.8 22.1 %all-to-all-start.2 = ((f32[128,1,512]{2,1,0:T(1,128)}), f32[128,1,512]{2,1,0:T(1,128)S(1)}, u32[]{:S(2)}, u32[]{:S(2)}) async-start(f32[128,1,512]{2,1,0:T(1,128)} %reshape.1452), calls=%async_computation.2 | async-start | bytes 524288 | tf_op jit(solution)/shard_map/all_to_all | solution.py:81
  100.0 8.9 collective-permute-start.5
  101.3 8.5 collective-permute-start.4
  109.9 13.8 %collective-permute-start.7 = (bf16[3,1,64,2048]{3,2,1,0:T(8,128)(2,1)S(1)}, bf16[3,1,64,2048]{3,2,1,0:T(8,128)(2,1)S(1)}, u32[]{:S(2)}, u32[]{:S(2)}) collective-permute-start(bf16[3,1,64,2048]{3,2,1,0:T(8,128)(2,1)S(1)} %pad_maximum_fusion.1), channel_id=1, source_target_pairs={{1,0},{2,1},{3,2},{4,3},{5,4},{6,5},{7,6},{9,8},{10,9},{11,10},{12... | collective-permute-start | bytes 2359304 | tf_op jit(solution)/shard_map/ppermute | solution.py:27
  113.8 11.0 collective-permute-start.6
  129.9 7.9 collective-permute-start.9
  131.2 8.0 collective-permute-start.8
  139.3 15.3 %collective-permute-start.11 = (bf16[3,1,64,2048]{3,2,1,0:T(8,128)(2,1)S(1)}, bf16[3,1,64,2048]{3,2,1,0:T(8,128)(2,1)S(1)}, u32[]{:S(2)}, u32[]{:S(2)}) collective-permute-start(bf16[3,1,64,2048]{3,2,1,0:T(8,128)(2,1)S(1)} %pad_maximum_fusion.2), channel_id=1, source_target_pairs={{1,0},{2,1},{3,2},{4,3},{5,4},{6,5},{7,6},{9,8},{10,9},{11,10},{12... | collective-permute-start | bytes 2359304 | tf_op jit(solution)/shard_map/ppermute | solution.py:27
  141.2 14.5 %collective-permute-start.10 = (bf16[3,1,64,2048]{3,2,1,0:T(8,128)(2,1)S(1)}, bf16[3,1,64,2048]{3,2,1,0:T(8,128)(2,1)S(1)}, u32[]{:S(2)}, u32[]{:S(2)}) collective-permute-start(bf16[3,1,64,2048]{3,2,1,0:T(8,128)(2,1)S(1)} %pad_maximum_fusion.2), channel_id=1, source_target_pairs={{0,1},{1,2},{2,3},{3,4},{4,5},{5,6},{6,7},{8,9},{9,10},{10,11},{11... | collective-permute-start | bytes 2359304 | tf_op jit(solution)/shard_map/ppermute | solution.py:25
  228.6 16.4 %all-to-all-start.3 = ((f32[128,1,512]{2,1,0:T(1,128)}), f32[128,1,512]{2,1,0:T(1,128)S(1)}, u32[]{:S(2)}, u32[]{:S(2)}) async-start(f32[128,1,512]{2,1,0:T(1,128)} %reshape.1454), calls=%async_computation.3 | async-start | bytes 524288 | tf_op jit(solution)/shard_map/all_to_all | solution.py:81
  248.4 8.9 collective-permute-start.13
  249.7 8.5 collective-permute-start.12
  258.3 13.8 %collective-permute-start.15 = (bf16[3,1,64,2048]{3,2,1,0:T(8,128)(2,1)S(1)}, bf16[3,1,64,2048]{3,2,1,0:T(8,128)(2,1)S(1)}, u32[]{:S(2)}, u32[]{:S(2)}) collective-permute-start(bf16[3,1,64,2048]{3,2,1,0:T(8,128)(2,1)S(1)} %pad_maximum_fusion.3), channel_id=1, source_target_pairs={{1,0},{2,1},{3,2},{4,3},{5,4},{6,5},{7,6},{9,8},{10,9},{11,10},{12... | collective-permute-start | bytes 2359304 | tf_op jit(solution)/shard_map/ppermute | solution.py:27
  262.2 11.0 collective-permute-start.14
  345.9 8.9 collective-permute-start.17
  347.2 8.4 collective-permute-start.16
  355.7 13.6 %collective-permute-start.19 = (bf16[3,1,64,2048]{3,2,1,0:T(8,128)(2,1)S(1)}, bf16[3,1,64,2048]{3,2,1,0:T(8,128)(2,1)S(1)}, u32[]{:S(2)}, u32[]{:S(2)}) collective-permute-start(bf16[3,1,64,2048]{3,2,1,0:T(8,128)(2,1)S(1)} %pad_maximum_fusion.4), channel_id=1, source_target_pairs={{1,0},{2,1},{3,2},{4,3},{5,4},{6,5},{7,6},{9,8},{10,9},{11,10},{12... | collective-permute-start | bytes 2359304 | tf_op jit(solution)/shard_map/ppermute | solution.py:27
  359.7 10.8 collective-permute-start.18
  442.3 16.5 %all-to-all-start.4 = ((f32[128,1,512]{2,1,0:T(1,128)}), f32[128,1,512]{2,1,0:T(1,128)S(1)}, u32[]{:S(2)}, u32[]{:S(2)}) async-start(f32[128,1,512]{2,1,0:T(1,128)} %reshape.1456), calls=%async_computation.4 | async-start | bytes 524288 | tf_op jit(solution)/shard_map/all_to_all | solution.py:81
  463.6 8.9 collective-permute-start.21
  464.9 8.5 collective-permute-start.20
  473.5 13.8 %collective-permute-start.23 = (bf16[3,1,64,2048]{3,2,1,0:T(8,128)(2,1)S(1)}, bf16[3,1,64,2048]{3,2,1,0:T(8,128)(2,1)S(1)}, u32[]{:S(2)}, u32[]{:S(2)}) collective-permute-start(bf16[3,1,64,2048]{3,2,1,0:T(8,128)(2,1)S(1)} %pad_maximum_fusion.5), channel_id=1, source_target_pairs={{1,0},{2,1},{3,2},{4,3},{5,4},{6,5},{7,6},{9,8},{10,9},{11,10},{12... | collective-permute-start | bytes 2359304 | tf_op jit(solution)/shard_map/ppermute | solution.py:27
  477.4 11.0 collective-permute-start.22
  563.1 8.6 collective-permute-start.25
  564.4 8.2 collective-permute-start.24
  572.7 13.7 %collective-permute-start.27 = (bf16[3,1,64,2048]{3,2,1,0:T(8,128)(2,1)S(1)}, bf16[3,1,64,2048]{3,2,1,0:T(8,128)(2,1)S(1)}, u32[]{:S(2)}, u32[]{:S(2)}) collective-permute-start(bf16[3,1,64,2048]{3,2,1,0:T(8,128)(2,1)S(1)} %pad_maximum_fusion.6), channel_id=1, source_target_pairs={{1,0},{2,1},{3,2},{4,3},{5,4},{6,5},{7,6},{9,8},{10,9},{11,10},{12... | collective-permute-start | bytes 2359304 | tf_op jit(solution)/shard_map/ppermute | solution.py:27
  576.9 10.8 collective-permute-start.26
  660.5 16.9 %all-to-all-start.5 = ((f32[128,1,512]{2,1,0:T(1,128)}), f32[128,1,512]{2,1,0:T(1,128)S(1)}, u32[]{:S(2)}, u32[]{:S(2)}) async-start(f32[128,1,512]{2,1,0:T(1,128)} %reshape.1458), calls=%async_computation.5 | async-start | bytes 524288 | tf_op jit(solution)/shard_map/all_to_all | solution.py:81
  682.2 8.9 collective-permute-start.29
  683.5 8.5 collective-permute-start.28
  692.1 13.8 %collective-permute-start.31 = (bf16[3,1,64,2048]{3,2,1,0:T(8,128)(2,1)S(1)}, bf16[3,1,64,2048]{3,2,1,0:T(8,128)(2,1)S(1)}, u32[]{:S(2)}, u32[]{:S(2)}) collective-permute-start(bf16[3,1,64,2048]{3,2,1,0:T(8,128)(2,1)S(1)} %pad_maximum_fusion.7), channel_id=1, source_target_pairs={{1,0},{2,1},{3,2},{4,3},{5,4},{6,5},{7,6},{9,8},{10,9},{11,10},{12... | collective-permute-start | bytes 2359304 | tf_op jit(solution)/shard_map/ppermute | solution.py:27
  696.0 11.0 collective-permute-start.30
  779.8 8.9 collective-permute-start.33
  781.1 8.5 collective-permute-start.32
  789.6 13.5 %collective-permute-start.35 = (bf16[3,1,64,2048]{3,2,1,0:T(8,128)(2,1)S(1)}, bf16[3,1,64,2048]{3,2,1,0:T(8,128)(2,1)S(1)}, u32[]{:S(2)}, u32[]{:S(2)}) collective-permute-start(bf16[3,1,64,2048]{3,2,1,0:T(8,128)(2,1)S(1)} %pad_maximum_fusion.8), channel_id=1, source_target_pairs={{1,0},{2,1},{3,2},{4,3},{5,4},{6,5},{7,6},{9,8},{10,9},{11,10},{12... | collective-permute-start | bytes 2359304 | tf_op jit(solution)/shard_map/ppermute | solution.py:27
  793.6 10.8 collective-permute-start.34
  876.2 16.5 %all-to-all-start.6 = ((f32[128,1,512]{2,1,0:T(1,128)}), f32[128,1,512]{2,1,0:T(1,128)S(1)}, u32[]{:S(2)}, u32[]{:S(2)}) async-start(f32[128,1,512]{2,1,0:T(1,128)} %reshape.1460), calls=%async_computation.6 | async-start | bytes 524288 | tf_op jit(solution)/shard_map/all_to_all | solution.py:81
  897.5 8.9 collective-permute-start.37
  898.8 8.5 collective-permute-start.36
  907.4 13.8 %collective-permute-start.39 = (bf16[3,1,64,2048]{3,2,1,0:T(8,128)(2,1)S(1)}, bf16[3,1,64,2048]{3,2,1,0:T(8,128)(2,1)S(1)}, u32[]{:S(2)}, u32[]{:S(2)}) collective-permute-start(bf16[3,1,64,2048]{3,2,1,0:T(8,128)(2,1)S(1)} %pad_maximum_fusion.9), channel_id=1, source_target_pairs={{1,0},{2,1},{3,2},{4,3},{5,4},{6,5},{7,6},{9,8},{10,9},{11,10},{12... | collective-permute-start | bytes 2359304 | tf_op jit(solution)/shard_map/ppermute | solution.py:27
  911.3 11.0 collective-permute-start.38
  996.9 8.9 collective-permute-start.41
  998.2 8.5 collective-permute-start.40
  1006.7 13.7 %collective-permute-start.43 = (bf16[3,1,64,2048]{3,2,1,0:T(8,128)(2,1)S(1)}, bf16[3,1,64,2048]{3,2,1,0:T(8,128)(2,1)S(1)}, u32[]{:S(2)}, u32[]{:S(2)}) collective-permute-start(bf16[3,1,64,2048]{3,2,1,0:T(8,128)(2,1)S(1)} %pad_maximum_fusion.10), channel_id=1, source_target_pairs={{1,0},{2,1},{3,2},{4,3},{5,4},{6,5},{7,6},{9,8},{10,9},{11,10},{12... | collective-permute-start | bytes 2359304 | tf_op jit(solution)/shard_map/ppermute | solution.py:27
  1010.7 10.9 collective-permute-start.42
  1093.2 16.6 %all-to-all-start.7 = ((f32[128,1,512]{2,1,0:T(1,128)}), f32[128,1,512]{2,1,0:T(1,128)S(1)}, u32[]{:S(2)}, u32[]{:S(2)}) async-start(f32[128,1,512]{2,1,0:T(1,128)} %reshape.1462), calls=%async_computation.7 | async-start | bytes 524288 | tf_op jit(solution)/shard_map/all_to_all | solution.py:81
  1114.6 8.9 collective-permute-start.45
  1115.9 8.5 collective-permute-start.44
  1124.5 13.8 %collective-permute-start.47 = (bf16[3,1,64,2048]{3,2,1,0:T(8,128)(2,1)S(1)}, bf16[3,1,64,2048]{3,2,1,0:T(8,128)(2,1)S(1)}, u32[]{:S(2)}, u32[]{:S(2)}) collective-permute-start(bf16[3,1,64,2048]{3,2,1,0:T(8,128)(2,1)S(1)} %pad_maximum_fusion.11), channel_id=1, source_target_pairs={{1,0},{2,1},{3,2},{4,3},{5,4},{6,5},{7,6},{9,8},{10,9},{11,10},{12... | collective-permute-start | bytes 2359304 | tf_op jit(solution)/shard_map/ppermute | solution.py:27
  1128.4 11.0 collective-permute-start.46
  1139.5 166.3 %copy-start.6 = (f32[64,512]{1,0:T(8,128)S(1)}, f32[64,512]{1,0:T(8,128)}, u32[]{:S(2)}) copy-start(f32[64,512]{1,0:T(8,128)} %copy-done.5) | copy-start | bytes 393220
  1139.5 166.3 %copy-start.8 = (f32[64,512]{1,0:T(8,128)S(1)}, f32[64,512]{1,0:T(8,128)}, u32[]{:S(2)}) copy-start(f32[64,512]{1,0:T(8,128)} %copy-done.7) | copy-start | bytes 393220
  1207.0 101.7 %copy-start.2 = (f32[64,512]{1,0:T(8,128)S(1)}, f32[64,512]{1,0:T(8,128)}, u32[]{:S(2)}) copy-start(f32[64,512]{1,0:T(8,128)} %copy-done.1) | copy-start | bytes 393220
  1207.0 101.7 %copy-start.4 = (f32[64,512]{1,0:T(8,128)S(1)}, f32[64,512]{1,0:T(8,128)}, u32[]{:S(2)}) copy-start(f32[64,512]{1,0:T(8,128)} %copy-done.3) | copy-start | bytes 393220
  1212.1 8.6 collective-permute-start.49
  1213.4 8.2 collective-permute-start.48
  1221.7 13.7 %collective-permute-start.51 = (bf16[3,1,64,2048]{3,2,1,0:T(8,128)(2,1)S(1)}, bf16[3,1,64,2048]{3,2,1,0:T(8,128)(2,1)S(1)}, u32[]{:S(2)}, u32[]{:S(2)}) collective-permute-start(bf16[3,1,64,2048]{3,2,1,0:T(8,128)(2,1)S(1)} %pad_maximum_fusion.12), channel_id=1, source_target_pairs={{1,0},{2,1},{3,2},{4,3},{5,4},{6,5},{7,6},{9,8},{10,9},{11,10},{12... | collective-permute-start | bytes 2359304 | tf_op jit(solution)/shard_map/ppermute | solution.py:27
  1225.9 10.8 collective-permute-start.50
  (39 other events, 1993.4 us)
